TPU v7x, 256 devices: a whole 4x4x8 slice. The times are simulated.
256 devices in a mesh: dp: 2 (over core), seq: 16 (over x, y), tensor: 8 (over z).
Axes of the slice: x: 4, y: 4, z: 8, core: 2. Of those that a mesh axis runs over, the one named last changes fastest.
Arguments:
- hidden: bfloat16 [16384, 7168], P(('dp', 'seq')), may hold values from -34 to 34
- grad_out: bfloat16 [16384, 4096], P(('dp', 'seq'), 'tensor'), may hold values from -24 to 24
- master_weight: float32 [7168, 4096], P(('dp', 'seq'), 'tensor'), may hold values from -6 to 6
- row_prev: float32 [7168], P(('dp', 'seq')), may hold values from 0.01 to 0.3
- col_prev: float32 [4096], P('tensor'), may hold values from 0.01 to 0.3
Outputs:
- new_weight: bfloat16 [7168, 4096], P('dp', 'tensor')
- update: float32 [7168, 4096], P(('dp', 'seq'), 'tensor')
- new_rows: float32 [7168], P(('dp', 'seq'))
- new_cols: float32 [4096], P('tensor')
All inputs are finite; a program needn't handle non-finite values.
Results may differ from a plain program's by a relative error of at most 0.0004.
Values may be sent and summed in bfloat16 or wider, within the bound.
A program may use at most 128 MiB of HBM per device.

v0:
```python
import jax
import jax.numpy as jnp
from jax import lax
from jax.sharding import PartitionSpec as P

D = 4096
FF_WIN = 7168
decay_rate = 0.8
learn_rate = 0.05
small_term = 1e-06


def per_device(hidden, grad_out, master_weight, row_prev, col_prev):
    grads = lax.psum_scatter(
        lax.dot_general(
            hidden, grad_out, (((0,), (0,)), ((), ())), preferred_element_type=jnp.float32
        ),
        ("dp", "seq"),
        scatter_dimension=0,
        tiled=True,
    )
    squares = grads * grads + small_term
    col_total = lax.psum(jnp.sum(squares, axis=0), ("dp", "seq"))
    row_total = lax.psum(jnp.sum(squares, axis=1), "tensor")
    new_rows = decay_rate * row_prev + (1.0 - decay_rate) * row_total / D
    new_cols = decay_rate * col_prev + (1.0 - decay_rate) * col_total / FF_WIN
    second = new_rows[:, None] * new_cols[None, :]
    raw = grads / jnp.sqrt(second)
    raw_total = lax.psum(jnp.sum(raw * raw), ("dp", "seq", "tensor"))
    size = jnp.sqrt(raw_total / (FF_WIN * D))
    update = raw / jnp.maximum(1.0, size)
    fresh = (master_weight - learn_rate * update).astype(jnp.bfloat16)
    new_weight = lax.all_gather(fresh, "seq", axis=0, tiled=True)
    return (new_weight, update, new_rows, new_cols)


def solution(mesh):
    return jax.shard_map(
        per_device,
        mesh=mesh,
        in_specs=(
            P(("dp", "seq"), None),
            P(("dp", "seq"), "tensor"),
            P(("dp", "seq"), "tensor"),
            P(("dp", "seq")),
            P("tensor"),
        ),
        out_specs=(P("dp", "tensor"), P(("dp", "seq"), "tensor"), P(("dp", "seq")), P("tensor")),
        check_vma=False,
    )
```

profile of v0, /device:TPU:1, one launch (start us, length us, event | category | flops | bytes accessed | tf_op | source)
XLA Modules:
  0.0 362.4 jit_solution(1551394529505662)
XLA Ops:
  7.2 0.0 copy-start
  7.2 0.0 reduce-scatter.2.cloned.1.call-start
  7.2 1.0 copy-done
  8.2 10.5 %fusion.4 = f32[7168,512]{1,0:T(8,128)} fusion(bf16[512,7168]{1,0:T(8,128)(2,1)} %param.5, bf16[512,512]{1,0:T(8,128)(2,1)S(1)} %copy-done), kind=kOutput, calls=%fused_computation.9 | convolution fusion | flops 3758096384 | bytes 22544384 | tf_op jit(solution)/shard_map/dot_general | solution.py:15
  18.7 0.0 copy-start.5
  18.7 0.0 copy-start.4
  18.7 0.0 copy-start.1
  18.7 0.0 reduce-scatter.2.cloned.1.call-update
  18.7 0.0 all-gather.2.cloned.1.call-start
  18.8 120.1 %reduce-scatter.2.cloned.1.call-done = f32[224,512]{1,0:T(8,128)} async-done(((f32[7168,512]{1,0:T(8,128)}), f32[224,512]{1,0:T(8,128)}) %reduce-scatter.2.cloned.1.call-update) | async-done | bytes 458768 | tf_op jit(solution)/shard_map/reduce_scatter | solution.py:14
  138.9 1.2 fusion.1
  140.0 13.7 %psum.21 = f32[224]{0:T(256)S(1)} all-reduce(f32[224]{0:T(256)S(1)} %get-tuple-element.4), channel_id=1, replica_groups=mesh['dp'=2,'seq'=16,'tensor'=8] {'tensor'}, use_global_device_ids=true, to_apply=%region_2.0 | all-reduce | flops 224 | bytes 1792 | tf_op jit(solution)/shard_map/psum | solution.py:24
  153.8 70.5 %psum.22 = f32[512]{0:T(512)S(1)} all-reduce(f32[512]{0:T(512)S(1)} %get-tuple-element.5), channel_id=1, replica_groups=mesh['dp'=2,'seq'=16,'tensor'=8] {'dp','seq'}, use_global_device_ids=true, to_apply=%region_4.0 | all-reduce | flops 512 | bytes 4096 | tf_op jit(solution)/shard_map/psum | solution.py:23
  224.3 0.0 copy-done.5
  224.3 0.0 copy-done.4
  224.3 0.0 copy-start.3
  224.4 0.0 copy-start.2
  224.4 1.8 multiply_reduce_fusion
  226.2 72.1 %psum.23 = f32[]{:T(128)} all-reduce(f32[]{:T(128)} %multiply_reduce_fusion), channel_id=1, replica_groups=mesh['dp'=2,'seq'=16,'tensor'=8] {'dp','seq','tensor'}, use_global_device_ids=true, to_apply=%region_6.0 | all-reduce | flops 1 | bytes 8 | tf_op jit(solution)/shard_map/psum | solution.py:29
  299.0 0.0 copy-done.1
  299.0 2.0 subtract_convert_fusion
  301.0 0.0 all-gather.2.cloned.1.call-update
  301.1 50.3 %all-gather.2.cloned.1.call-done = bf16[3584,512]{1,0:T(8,128)(2,1)} async-done(((bf16[224,512]{1,0:T(8,128)(2,1)}), bf16[3584,512]{1,0:T(8,128)(2,1)}) %all-gather.2.cloned.1.call-update) | async-done | bytes 3670032 | tf_op jit(solution)/shard_map/all_gather | solution.py:33
  351.4 4.1 %copy.10 = bf16[3584,512]{1,0:T(8,128)(2,1)} copy(bf16[3584,512]{1,0:T(8,128)(2,1)} %all-gather.2.cloned.1.call-done) | data formatting | bytes 7340032
  355.5 0.0 copy-done.3
  355.5 0.0 copy-done.2
  (2 shorter events, 0.0 us)
Async XLA Ops:
  7.2 1.0 copy-start
  7.2 131.7 %reduce-scatter.2.cloned.1.call-start = ((), (), s32[]{:S(2)}) async-start(), calls=%async_computation.1 | async-start | bytes 15138816 | tf_op jit(solution)/shard_map/reduce_scatter | solution.py:14
  18.7 205.6 %copy-start.5 = (f32[224]{0:T(256)S(1)}, f32[224]{0:T(256)}, u32[]{:S(2)}) copy-start(f32[224]{0:T(256)} %param.8) | copy-start | bytes 2692
  18.7 205.6 %copy-start.4 = (f32[512]{0:T(512)S(1)}, f32[512]{0:T(512)}, u32[]{:S(2)}) copy-start(f32[512]{0:T(512)} %param.9) | copy-start | bytes 6148
  18.7 280.3 %copy-start.1 = (f32[224,512]{1,0:T(8,128)S(1)}, f32[224,512]{1,0:T(8,128)}, u32[]{:S(2)}) copy-start(f32[224,512]{1,0:T(8,128)} %param.7) | copy-start | bytes 1376260
  18.7 332.7 %all-gather.2.cloned.1.call-start = ((), (), s32[]{:S(2)}) async-start(), calls=%async_computation.2 | async-start | bytes 3899392 | tf_op jit(solution)/shard_map/all_gather | solution.py:33
  224.3 131.2 %copy-start.3 = (f32[224]{0:T(256)}, f32[224]{0:T(256)S(1)}, u32[]{:S(2)}) copy-start(f32[224]{0:T(256)S(1)} %multiply_add_fusion.2) | copy-start | bytes 2692
  224.4 131.1 %copy-start.2 = (f32[512]{0:T(512)}, f32[512]{0:T(512)S(1)}, u32[]{:S(2)}) copy-start(f32[512]{0:T(512)S(1)} %multiply_add_fusion.1) | copy-start | bytes 6148
Sparse Core Ops, SparseCore 0:
  18.8 119.9 reduce-scatter.1
  301.2 50.1 all-gather.1
where the time goes:
time: 363 us; the launch traced here: 362 us
  waiting for transfers between devices  170 us (47%)
  blocking collectives  156 us (43%)
  between operations  14.8 us (4%)
  matrix products  10.5 us (3%)
  local copies, waits for them, and re-layouts  5.13 us (1%)
  other arithmetic  5.03 us (1%)
    reduce_scatter x1, waiting for transfers between devices, per_device(): lax.psum_scatter(lax.dot_general(hidden, grad_out, (((0,), (0,)), ((), ()...  120 us
    psum x1, blocking collectives, per_device(): raw_total = lax.psum(jnp.sum(raw * raw), ('dp', 'seq', 'tensor'))  72.1 us
    psum x1, blocking collectives, per_device(): col_total = lax.psum(jnp.sum(squares, axis=0), ('dp', 'seq'))  70.5 us
    all_gather x1, waiting for transfers between devices, per_device(): new_weight = lax.all_gather(fresh, 'seq', axis=0, tiled=True)  50.3 us
    psum x1, blocking collectives, per_device(): row_total = lax.psum(jnp.sum(squares, axis=1), 'tensor')  13.7 us
    dot_general x1, matrix products, per_device(): lax.dot_general(hidden, grad_out, (((0,), (0,)), ((), ())), preferred_ele...  10.5 us
  transfers between devices with their start and end apart: 2, of which 2 were waited for; matrix products, arithmetic and copies ran while one was open for 0% of the time, Pallas kernels for 0%

commit v1 on v0

--- a/solution.py
+++ b/solution.py
@@ -21,7 +21,7 @@
     )
     squares = grads * grads + small_term
     col_total = lax.psum(jnp.sum(squares, axis=0), ("dp", "seq"))
-    row_total = lax.psum(jnp.sum(squares, axis=1), "tensor")
+    row_total = jnp.sum(lax.all_gather(jnp.sum(squares, axis=1), "tensor"), axis=0)
     new_rows = decay_rate * row_prev + (1.0 - decay_rate) * row_total / D
     new_cols = decay_rate * col_prev + (1.0 - decay_rate) * col_total / FF_WIN
     second = new_rows[:, None] * new_cols[None, :]

time: 363 us -> 363 us (level)
    unnamed x0 -> x1, blocking collectives: none -> 13.9 us
    psum x1 -> x0, blocking collectives: 13.7 us -> none  [per_device(): row_total = lax.psum(jnp.sum(squares, axis=1), 'tensor')]
where the time goes in v1:
time: 363 us
  waiting for transfers between devices  169 us (47%)
  blocking collectives  157 us (43%)
  between operations  15.5 us (4%)
  matrix products  10.5 us (3%)
  local copies, waits for them, and re-layouts  6.65 us (2%)
  other arithmetic  5.06 us (1%)
    reduce_scatter x1, waiting for transfers between devices, per_device(): lax.psum_scatter(lax.dot_general(hidden, grad_out, (((0,), (0,)), ((), ()...  118 us
    psum x1, blocking collectives, per_device(): raw_total = lax.psum(jnp.sum(raw * raw), ('dp', 'seq', 'tensor'))  72.1 us
    psum x1, blocking collectives, per_device(): col_total = lax.psum(jnp.sum(squares, axis=0), ('dp', 'seq'))  70.6 us
    all_gather x1, waiting for transfers between devices, per_device(): new_weight = lax.all_gather(fresh, 'seq', axis=0, tiled=True)  50.3 us
    unnamed x1, blocking collectives  13.9 us
    dot_general x1, matrix products, per_device(): lax.dot_general(hidden, grad_out, (((0,), (0,)), ((), ())), preferred_ele...  10.5 us
  transfers between devices with their start and end apart: 2, of which 2 were waited for; matrix products, arithmetic and copies ran while one was open for 0% of the time, Pallas kernels for 0%

profile of v1, /device:TPU:1, one launch (start us, length us, event | category | flops | bytes accessed | tf_op | source)
XLA Modules:
  0.0 363.0 jit_solution(14424026349936314652)
XLA Ops:
  7.2 0.0 copy-start
  7.2 0.0 reduce-scatter.2.cloned.1.call-start
  7.2 1.0 copy-done
  8.2 10.5 %fusion.4 = f32[7168,512]{1,0:T(8,128)} fusion(bf16[512,7168]{1,0:T(8,128)(2,1)} %param.5, bf16[512,512]{1,0:T(8,128)(2,1)S(1)} %copy-done), kind=kOutput, calls=%fused_computation.9 | convolution fusion | flops 3758096384 | bytes 22544384 | tf_op jit(solution)/shard_map/dot_general | solution.py:15
  18.7 0.0 copy-start.6
  18.7 0.0 copy-start.5
  18.7 0.0 copy-start.4
  18.7 0.0 copy-start.1
  18.7 0.0 reduce-scatter.2.cloned.1.call-update
  18.7 0.0 all-gather.3.cloned.1.call-start
  18.8 0.6 copy-done.6
  19.4 0.6 dynamic-slice
  20.6 118.3 %reduce-scatter.2.cloned.1.call-done = f32[224,512]{1,0:T(8,128)} async-done(((f32[7168,512]{1,0:T(8,128)}), f32[224,512]{1,0:T(8,128)}) %reduce-scatter.2.cloned.1.call-update) | async-done | bytes 458768 | tf_op jit(solution)/shard_map/reduce_scatter | solution.py:14
  138.9 1.2 fusion.1
  140.1 0.3 dynamic-update-slice
  140.3 13.9 %all-reduce = f32[1792]{0:T(1024)S(1)} all-reduce(f32[1792]{0:T(1024)S(1)} %dynamic-update-slice), channel_id=2, replica_groups=mesh['dp'=2,'seq'=16,'tensor'=8] {'tensor'}, use_global_device_ids=true, to_apply=%add | all-reduce | flops 1792 | bytes 14336
  154.2 0.1 reshape.10
  154.3 70.6 %psum.14 = f32[512]{0:T(512)S(1)} all-reduce(f32[512]{0:T(512)S(1)} %get-tuple-element.5), channel_id=1, replica_groups=mesh['dp'=2,'seq'=16,'tensor'=8] {'dp','seq'}, use_global_device_ids=true, to_apply=%region_4.0 | all-reduce | flops 512 | bytes 4096 | tf_op jit(solution)/shard_map/psum | solution.py:23
  224.9 0.0 copy-done.5
  225.0 0.0 copy-done.4
  225.0 0.0 copy-start.3
  225.0 0.0 copy-start.2
  225.0 1.8 multiply_reduce_fusion
  226.8 72.1 %psum.15 = f32[]{:T(128)} all-reduce(f32[]{:T(128)} %multiply_reduce_fusion), channel_id=1, replica_groups=mesh['dp'=2,'seq'=16,'tensor'=8] {'dp','seq','tensor'}, use_global_device_ids=true, to_apply=%region_6.0 | all-reduce | flops 1 | bytes 8 | tf_op jit(solution)/shard_map/psum | solution.py:29
  299.6 0.0 copy-done.1
  299.6 2.0 subtract_convert_fusion
  301.7 0.0 all-gather.3.cloned.1.call-update
  301.7 50.3 %all-gather.3.cloned.1.call-done = bf16[3584,512]{1,0:T(8,128)(2,1)} async-done(((bf16[224,512]{1,0:T(8,128)(2,1)}), bf16[3584,512]{1,0:T(8,128)(2,1)}) %all-gather.3.cloned.1.call-update) | async-done | bytes 3670032 | tf_op jit(solution)/shard_map/all_gather | solution.py:33
  352.0 4.1 %copy.11 = bf16[3584,512]{1,0:T(8,128)(2,1)} copy(bf16[3584,512]{1,0:T(8,128)(2,1)} %all-gather.3.cloned.1.call-done) | data formatting | bytes 7340032
  356.1 0.0 copy-done.3
  356.1 0.0 copy-done.2
  (4 shorter events, 0.0 us)
Async XLA Ops:
  7.2 1.0 copy-start
  7.2 131.7 %reduce-scatter.2.cloned.1.call-start = ((), (), s32[]{:S(2)}) async-start(), calls=%async_computation.1 | async-start | bytes 15138816 | tf_op jit(solution)/shard_map/reduce_scatter | solution.py:14
  18.7 0.7 copy-start.6
  18.7 206.2 %copy-start.5 = (f32[224]{0:T(256)S(1)}, f32[224]{0:T(256)}, u32[]{:S(2)}) copy-start(f32[224]{0:T(256)} %param.8) | copy-start | bytes 2692
  18.7 206.3 %copy-start.4 = (f32[512]{0:T(512)S(1)}, f32[512]{0:T(512)}, u32[]{:S(2)}) copy-start(f32[512]{0:T(512)} %param.9) | copy-start | bytes 6148
  18.7 280.9 %copy-start.1 = (f32[224,512]{1,0:T(8,128)S(1)}, f32[224,512]{1,0:T(8,128)}, u32[]{:S(2)}) copy-start(f32[224,512]{1,0:T(8,128)} %param.7) | copy-start | bytes 1376260
  18.7 333.3 %all-gather.3.cloned.1.call-start = ((), (), s32[]{:S(2)}) async-start(), calls=%async_computation.2 | async-start | bytes 3899392 | tf_op jit(solution)/shard_map/all_gather | solution.py:33
  225.0 131.2 %copy-start.3 = (f32[224]{0:T(256)}, f32[224]{0:T(256)S(1)}, u32[]{:S(2)}) copy-start(f32[224]{0:T(256)S(1)} %multiply_add_fusion.2) | copy-start | bytes 2692
  225.0 131.2 %copy-start.2 = (f32[512]{0:T(512)}, f32[512]{0:T(512)S(1)}, u32[]{:S(2)}) copy-start(f32[512]{0:T(512)S(1)} %multiply_add_fusion.1) | copy-start | bytes 6148
Sparse Core Ops, SparseCore 0:
  18.9 119.9 reduce-scatter.1
  301.8 50.1 all-gather.2

commit v2 on v0

--- a/solution.py
+++ b/solution.py
@@ -20,7 +20,7 @@
         tiled=True,
     )
     squares = grads * grads + small_term
-    col_total = lax.psum(jnp.sum(squares, axis=0), ("dp", "seq"))
+    col_total = lax.psum(lax.psum(jnp.sum(squares, axis=0), "seq"), "dp")
     row_total = lax.psum(jnp.sum(squares, axis=1), "tensor")
     new_rows = decay_rate * row_prev + (1.0 - decay_rate) * row_total / D
     new_cols = decay_rate * col_prev + (1.0 - decay_rate) * col_total / FF_WIN

time: 363 us -> 339 us (0.934)
  blocking collectives: 156 us -> 132 us
    psum x1 -> x2, blocking collectives: 70.5 us -> 45.8 us  [per_device(): col_total = lax.psum(lax.psum(jnp.sum(squares, axis=0), 'seq'), 'dp')]
where the time goes in v2:
time: 339 us; the launch traced here: 338 us
  waiting for transfers between devices  170 us (50%)
  blocking collectives  132 us (39%)
  between operations  14.8 us (4%)
  matrix products  10.5 us (3%)
  local copies, waits for them, and re-layouts  5.13 us (2%)
  other arithmetic  5.03 us (1%)
    reduce_scatter x1, waiting for transfers between devices, per_device(): lax.psum_scatter(lax.dot_general(hidden, grad_out, (((0,), (0,)), ((), ()...  120 us
    psum x1, blocking collectives, per_device(): raw_total = lax.psum(jnp.sum(raw * raw), ('dp', 'seq', 'tensor'))  72.7 us
    all_gather x1, waiting for transfers between devices, per_device(): new_weight = lax.all_gather(fresh, 'seq', axis=0, tiled=True)  50.3 us
    psum x2, blocking collectives, per_device(): col_total = lax.psum(lax.psum(jnp.sum(squares, axis=0), 'seq'), 'dp')  45.8 us
    psum x1, blocking collectives, per_device(): row_total = lax.psum(jnp.sum(squares, axis=1), 'tensor')  13.7 us
    dot_general x1, matrix products, per_device(): lax.dot_general(hidden, grad_out, (((0,), (0,)), ((), ())), preferred_ele...  10.5 us
  transfers between devices with their start and end apart: 2, of which 2 were waited for; matrix products, arithmetic and copies ran while one was open for 0% of the time, Pallas kernels for 0%

profile of v2, /device:TPU:1, one launch (start us, length us, event | category | flops | bytes accessed | tf_op | source)
XLA Modules:
  0.0 338.2 jit_solution(11403570304043887320)
XLA Ops:
  7.2 0.0 copy-start
  7.2 0.0 reduce-scatter.2.cloned.1.call-start
  7.2 1.0 copy-done
  8.2 10.5 %fusion.4 = f32[7168,512]{1,0:T(8,128)} fusion(bf16[512,7168]{1,0:T(8,128)(2,1)} %param.5, bf16[512,512]{1,0:T(8,128)(2,1)S(1)} %copy-done), kind=kOutput, calls=%fused_computation.9 | convolution fusion | flops 3758096384 | bytes 22544384 | tf_op jit(solution)/shard_map/dot_general | solution.py:15
  18.7 0.0 copy-start.5
  18.7 0.0 copy-start.4
  18.7 0.0 copy-start.1
  18.7 0.0 reduce-scatter.2.cloned.1.call-update
  18.7 0.0 all-gather.2.cloned.1.call-start
  18.8 120.1 %reduce-scatter.2.cloned.1.call-done = f32[224,512]{1,0:T(8,128)} async-done(((f32[7168,512]{1,0:T(8,128)}), f32[224,512]{1,0:T(8,128)}) %reduce-scatter.2.cloned.1.call-update) | async-done | bytes 458768 | tf_op jit(solution)/shard_map/reduce_scatter | solution.py:14
  138.9 1.2 fusion.1
  140.0 13.7 %psum.28 = f32[224]{0:T(256)S(1)} all-reduce(f32[224]{0:T(256)S(1)} %get-tuple-element.4), channel_id=1, replica_groups=mesh['dp'=2,'seq'=16,'tensor'=8] {'tensor'}, use_global_device_ids=true, to_apply=%region_2.0 | all-reduce | flops 224 | bytes 1792 | tf_op jit(solution)/shard_map/psum | solution.py:24
  153.8 30.9 %psum.29 = f32[512]{0:T(512)S(1)} all-reduce(f32[512]{0:T(512)S(1)} %get-tuple-element.5), channel_id=1, replica_groups=mesh['dp'=2,'seq'=16,'tensor'=8] {'seq'}, use_global_device_ids=true, to_apply=%region_4.0 | all-reduce | flops 512 | bytes 4096 | tf_op jit(solution)/shard_map/psum | solution.py:23
  184.7 14.9 %psum.30 = f32[512]{0:T(512)S(1)} all-reduce(f32[512]{0:T(512)S(1)} %psum.29), channel_id=1, replica_groups=mesh['dp'=2,'seq'=16,'tensor'=8] {'dp'}, use_global_device_ids=true, to_apply=%region_5.0 | all-reduce | flops 512 | bytes 4096 | tf_op jit(solution)/shard_map/psum | solution.py:23
  199.6 0.0 copy-done.5
  199.6 0.0 copy-done.4
  199.6 0.0 copy-start.3
  199.7 0.0 copy-start.2
  199.7 1.8 multiply_reduce_fusion
  201.5 72.7 %psum.31 = f32[]{:T(128)} all-reduce(f32[]{:T(128)} %multiply_reduce_fusion), channel_id=1, replica_groups=mesh['dp'=2,'seq'=16,'tensor'=8] {'dp','seq','tensor'}, use_global_device_ids=true, to_apply=%region_7.0 | all-reduce | flops 1 | bytes 8 | tf_op jit(solution)/shard_map/psum | solution.py:29
  274.9 0.0 copy-done.1
  274.9 2.0 subtract_convert_fusion
  276.9 0.0 all-gather.2.cloned.1.call-update
  276.9 50.3 %all-gather.2.cloned.1.call-done = bf16[3584,512]{1,0:T(8,128)(2,1)} async-done(((bf16[224,512]{1,0:T(8,128)(2,1)}), bf16[3584,512]{1,0:T(8,128)(2,1)}) %all-gather.2.cloned.1.call-update) | async-done | bytes 3670032 | tf_op jit(solution)/shard_map/all_gather | solution.py:33
  327.2 4.1 %copy.10 = bf16[3584,512]{1,0:T(8,128)(2,1)} copy(bf16[3584,512]{1,0:T(8,128)(2,1)} %all-gather.2.cloned.1.call-done) | data formatting | bytes 7340032
  331.3 0.0 copy-done.3
  331.3 0.0 copy-done.2
  (2 shorter events, 0.0 us)
Async XLA Ops:
  7.2 1.0 copy-start
  7.2 131.7 %reduce-scatter.2.cloned.1.call-start = ((), (), s32[]{:S(2)}) async-start(), calls=%async_computation.1 | async-start | bytes 15138816 | tf_op jit(solution)/shard_map/reduce_scatter | solution.py:14
  18.7 180.9 %copy-start.5 = (f32[224]{0:T(256)S(1)}, f32[224]{0:T(256)}, u32[]{:S(2)}) copy-start(f32[224]{0:T(256)} %param.8) | copy-start | bytes 2692
  18.7 180.9 %copy-start.4 = (f32[512]{0:T(512)S(1)}, f32[512]{0:T(512)}, u32[]{:S(2)}) copy-start(f32[512]{0:T(512)} %param.9) | copy-start | bytes 6148
  18.7 256.2 %copy-start.1 = (f32[224,512]{1,0:T(8,128)S(1)}, f32[224,512]{1,0:T(8,128)}, u32[]{:S(2)}) copy-start(f32[224,512]{1,0:T(8,128)} %param.7) | copy-start | bytes 1376260
  18.7 308.5 %all-gather.2.cloned.1.call-start = ((), (), s32[]{:S(2)}) async-start(), calls=%async_computation.2 | async-start | bytes 3899392 | tf_op jit(solution)/shard_map/all_gather | solution.py:33
  199.6 131.7 %copy-start.3 = (f32[224]{0:T(256)}, f32[224]{0:T(256)S(1)}, u32[]{:S(2)}) copy-start(f32[224]{0:T(256)S(1)} %multiply_add_fusion.2) | copy-start | bytes 2692
  199.7 131.7 %copy-start.2 = (f32[512]{0:T(512)}, f32[512]{0:T(512)S(1)}, u32[]{:S(2)}) copy-start(f32[512]{0:T(512)S(1)} %multiply_add_fusion.1) | copy-start | bytes 6148
Sparse Core Ops, SparseCore 0:
  18.8 119.9 reduce-scatter.1
  277.0 50.1 all-gather.1
